TPU v7x, 256 devices: a whole 4x4x8 slice. The times are simulated.
256 devices in a mesh: ka: 32 (over y_hi, z, core), band: 8 (over y_lo, x).
Axes of the slice: x: 4, y: 4 (y_hi: 2, y_lo: 2; y = y_hi * 2 + y_lo), z: 8, core: 2. Of those that a mesh axis runs over, the one named last changes fastest.
Arguments:
- coefficients: bfloat16 [32, 2, 160, 2400], P('ka'), may hold values from -6 to 6
- class_weight: float32 [32], replicated, may hold values from 0.5 to 5
- diff_class: int32 [32, 32], replicated, may hold values from 0 to 31
- frag_cells: int32 [2], replicated, may hold values from 0 to 31
- block_pattern: int32 [2, 30], replicated, may hold values 0 or 1
Outputs:
- cluster: float32 [2, 2, 160, 2400], P(None, None, 'band', 'ka')
All inputs are finite; a program needn't handle non-finite values.
Results may differ from a plain program's by a relative error of at most 0.0017.
Values may be sent and summed in bfloat16 or wider, within the bound.
No kernel may reach another device: no remote copies, remote signals or barrier semaphores. Data moves between devices by JAX's collectives and lax.ppermute only.
A program may use at most 64 MiB of HBM per device.

v0:
```python
import jax
import jax.numpy as jnp
from jax import lax
from jax.sharding import PartitionSpec as P


def shards(coefficients, class_weight, diff_class, frag_cells, block_pattern):
    own_block = coefficients[0]
    occupied = own_block.shape[1]
    functions = own_block.shape[2]
    band_count = lax.axis_size("band")
    group_width = occupied // band_count
    kpoint_count = lax.axis_size("ka")
    kpoint_index = lax.axis_index("ka")
    high = lax.Precision.HIGHEST
    own_flat = own_block.reshape(2 * occupied, functions)
    my_group = lax.dynamic_slice_in_dim(
        own_block, lax.axis_index("band") * group_width, group_width, 1
    )
    diff_row = lax.dynamic_index_in_dim(diff_class, kpoint_index, 0, keepdims=False)
    classes = jnp.arange(class_weight.shape[0], dtype=jnp.int32)
    onehot = (diff_row[:, None] == classes[None, :]).astype(jnp.float32)
    weights = jnp.dot(onehot, class_weight, precision=high) / functions
    piece = lax.all_gather(my_group[None], "ka", axis=0, tiled=True)
    pieces = piece.shape[0]
    blocks = piece.reshape(pieces, 2 * group_width, functions)
    intersection = jnp.einsum("qia,ja->qij", blocks, own_flat, preferred_element_type=jnp.float32)
    m_real = intersection[:, :group_width, :occupied] + intersection[:, group_width:, occupied:]
    m_imag = intersection[:, :group_width, occupied:] - intersection[:, group_width:, :occupied]
    scaling = weights[:, None, None]
    m_real = (scaling * m_real).astype(jnp.bfloat16)
    m_imag = (scaling * m_imag).astype(jnp.bfloat16)
    m_block = jnp.concatenate(
        [jnp.concatenate([m_real, m_imag], 2), jnp.concatenate([-m_imag, m_real], 2)], 1
    )
    exchange = jnp.einsum("qio,qia->oa", m_block, blocks, preferred_element_type=jnp.float32)
    exchange = exchange.reshape(2, occupied, functions)
    phase_index = kpoint_index * frag_cells % kpoint_count
    angles = 2.0 * jnp.pi * phase_index.astype(jnp.float32) / kpoint_count
    cosines = (jnp.cos(angles) / kpoint_count)[:, None, None]
    sines = (jnp.sin(angles) / kpoint_count)[:, None, None]
    w_real = exchange[0][None]
    w_imag = exchange[1][None]
    terms = jnp.stack([cosines * w_real - sines * w_imag, sines * w_real + cosines * w_imag], 1)
    partial_value = lax.psum_scatter(terms, "band", scatter_dimension=2, tiled=True)
    cluster = lax.psum_scatter(partial_value, "ka", scatter_dimension=3, tiled=True)
    columns = cluster.shape[3]
    block_size = functions // block_pattern.shape[1]
    local_ids = (kpoint_index * columns + jnp.arange(columns, dtype=jnp.int32)) // block_size
    block_ids = jnp.arange(block_pattern.shape[1], dtype=jnp.int32)
    block_onehot = (block_ids[:, None] == local_ids[None, :]).astype(jnp.float32)
    block_mask = jnp.dot(block_pattern.astype(jnp.float32), block_onehot, precision=high)
    return cluster * block_mask[:, None, None, :]


def solution(mesh):
    placed = (P("ka", None, None, None), P(), P(), P(), P())
    return jax.shard_map(
        shards, mesh=mesh, in_specs=placed, out_specs=P(None, None, "band", "ka"), check_vma=False
    )
```

profile of v0, /device:TPU:1, one launch (start us, length us, event | category | flops | bytes accessed | tf_op | source)
XLA Modules:
  0.0 558.0 jit_solution(7503871566022568461)
XLA Ops:
  6.5 0.0 copy-start
  6.5 0.0 all-gather.2.cloned.1.call-start
  6.5 1.4 copy-done
  7.9 0.1 constant_dynamic-slice_fusion.1
  8.0 0.8 copy.19
  8.8 0.0 all-gather.2.cloned.1.call-update
  8.8 0.0 all-reduce.5.cloned.1.call-start
  8.9 0.7 dynamic-slice_bitcast_fusion
  9.6 0.7 cosine_multiply_fusion
  10.4 0.8 fusion
  11.2 97.5 %all-gather.2.cloned.1.call-done = bf16[32,2,20,2400]{3,1,2,0:T(2,128)(2,1)} async-done(((bf16[1,2,20,2400]{3,1,2,0:T(2,128)(2,1)}), bf16[32,2,20,2400]{3,1,2,0:T(2,128)(2,1)}) %all-gather.2.cloned.1.call-update) | async-done | bytes 6144016 | tf_op jit(solution)/shard_map/all_gather | solution.py:24
  108.7 3.5 copy.10
  112.2 3.5 fusion.24
  115.7 0.3 fusion.11
  116.0 0.3 fusion.21
  116.2 2.5 convolution_bitcast_fusion
  118.7 0.2 fusion.23
  118.9 6.8 %multiply_subtract_fusion = (f32[2,1,160,2400]{3,1,2,0:T(1,128)S(1)}, f32[2,1,160,2400]{3,1,2,0:T(1,128)}) fusion(f32[160,2400]{1,0:T(8,128)S(1)} %get-tuple-element.12, f32[160,2400]{1,0:T(8,128)S(1)} %get-tuple-element.11, f32[2]{0:T(128)S(1)} %sine_multiply_fusion, f32[2]{0:T(128)S(1)} %get-tuple-element.5), kind=kLoop, calls=%fused_computation.3 | loop fusion | flops 4608000 | bytes 9216016 | tf_op jit(solution)/shard_map/sub | solution.py:44
  125.7 10.2 %pad_maximum_fusion = f32[2,2,160,2400]{3,1,2,0:T(2,128)} fusion(f32[2,1,160,2400]{3,1,2,0:T(1,128)} %get-tuple-element.10, f32[2,1,160,2400]{3,1,2,0:T(1,128)S(1)} %get-tuple-element.9), kind=kLoop, calls=%fused_computation | loop fusion | flops 1536000 | bytes 12288000 | tf_op jit(solution)/shard_map/stack | solution.py:44
  135.9 0.0 copy-start.3
  135.9 0.0 copy-start.2
  135.9 0.0 copy-start.1
  135.9 0.0 all-reduce.5.cloned.1.call-update
  135.9 0.0 all-reduce.7.cloned.1.call-start
  136.0 0.6 copy-done.3
  136.6 0.6 dynamic-slice.1
  137.8 143.1 %all-reduce.5.cloned.1.call-done = f32[2,2,160,2400]{3,1,2,0:T(2,128)} async-done(((f32[2,2,160,2400]{3,1,2,0:T(2,128)}), f32[2,2,160,2400]{3,1,2,0:T(2,128)}) %all-reduce.5.cloned.1.call-update) | async-done | bytes 6144016
  280.9 2.1 constant_dynamic-slice_fusion
  283.0 0.0 all-reduce.7.cloned.1.call-update
  283.0 0.0 copy-done.2
  283.0 0.6 dynamic-slice.3
  284.3 0.0 copy-done.1
  284.3 0.1 convolution_bitcast_fusion.1
  284.4 265.5 %all-reduce.7.cloned.1.call-done = f32[2,2,20,2400]{3,1,2,0:T(2,128)} async-done(((f32[2,2,20,2400]{3,1,2,0:T(2,128)}), f32[2,2,20,2400]{3,1,2,0:T(2,128)}) %all-reduce.7.cloned.1.call-update) | async-done | bytes 768016
  549.9 1.6 dynamic-slice_multiply_fusion
  (2 shorter events, 0.1 us)
Async XLA Ops:
  6.5 1.4 copy-start
  6.5 102.2 %all-gather.2.cloned.1.call-start = ((), (), s32[]{:S(2)}) async-start(), calls=%async_computation | async-start | bytes 6420480 | tf_op jit(solution)/shard_map/all_gather | solution.py:24
  8.8 272.0 %all-reduce.5.cloned.1.call-start = ((), (), s32[]{:S(2)}) async-start(), calls=%async_computation.1 | async-start | bytes 12451840
  135.9 0.7 copy-start.3
  135.9 147.1 %copy-start.2 = (u32[256]{0:T(256)S(1)}, u32[256]{0:T(256)}, u32[]{:S(2)}) copy-start(u32[256]{0:T(256)} %constant.64) | copy-start | bytes 3076
  135.9 148.4 %copy-start.1 = (s32[2,30]{1,0:T(2,128)S(1)}, s32[2,30]{1,0:T(2,128)}, u32[]{:S(2)}) copy-start(s32[2,30]{1,0:T(2,128)} %param.9) | copy-start | bytes 724
  135.9 414.0 %all-reduce.7.cloned.1.call-start = ((), (), s32[]{:S(2)}) async-start(), calls=%async_computation.2 | async-start | bytes 1556480
Sparse Core Ops, SparseCore 0:
  10.1 98.5 all-gather.1
  136.0 144.7 all-reduce.4
  283.7 266.1 all-reduce.6
where the time goes:
time: 558 us
  waiting for transfers between devices  506 us (91%)
  other arithmetic  19.9 us (4%)
  between operations  14.5 us (3%)
  local copies, waits for them, and re-layouts  10.5 us (2%)
  matrix products  6.93 us (1%)
    unnamed x5, waiting for transfers between devices  409 us
    all_gather x1, waiting for transfers between devices, shards(): piece = lax.all_gather(my_group[None], 'ka', axis=0, tiled=True)  97.5 us
  transfers between devices with their start and end apart: 3, of which 3 were waited for; matrix products, arithmetic and copies ran while one was open for 1% of the time, Pallas kernels for 0%

commit v1 on v0

--- a/solution.py
+++ b/solution.py
@@ -21,7 +21,9 @@
     classes = jnp.arange(class_weight.shape[0], dtype=jnp.int32)
     onehot = (diff_row[:, None] == classes[None, :]).astype(jnp.float32)
     weights = jnp.dot(onehot, class_weight, precision=high) / functions
-    piece = lax.all_gather(my_group[None], "ka", axis=0, tiled=True)
+    piece = jnp.concatenate(
+        lax.all_to_all(jnp.stack([my_group[None]] * lax.axis_size("ka")), "ka", 0, 0), axis=0
+    )
     pieces = piece.shape[0]
     blocks = piece.reshape(pieces, 2 * group_width, functions)
     intersection = jnp.einsum("qia,ja->qij", blocks, own_flat, preferred_element_type=jnp.float32)

time: 558 us -> 619 us (1.11)
  waiting for transfers between devices: 506 us -> 551 us
  starting transfers between devices: 0.09 us -> 13 us
    all_to_all x0 -> x1, waiting for transfers between devices: none -> 138 us  [shards(): lax.all_to_all(jnp.stack([my_group[None]] * lax.axis_size('ka')), 'ka', 0...]
    all_gather x1 -> x0, waiting for transfers between devices: 97.5 us -> none  [shards(): piece = lax.all_gather(my_group[None], 'ka', axis=0, tiled=True)]
    all_to_all x0 -> x1, starting transfers between devices: none -> 12.9 us  [shards(): lax.all_to_all(jnp.stack([my_group[None]] * lax.axis_size('ka')), 'ka', 0...]
    unnamed x5 -> x4, waiting for transfers between devices: 409 us -> 412 us
  transfers between devices with their start and end apart: 3 -> 3, of which waited for: 3 -> 3; matrix products, arithmetic and copies ran while one was open for 1% -> 0% of each run, Pallas kernels for 0% -> 0%
where the time goes in v1:
time: 619 us; the launch traced here: 618 us
  waiting for transfers between devices  551 us (89%)
  other arithmetic  19.2 us (3%)
  between operations  14.8 us (2%)
  local copies, waits for them, and re-layouts  14.3 us (2%)
  starting transfers between devices  13 us (2%)
  matrix products  6.27 us (1%)
    unnamed x4, waiting for transfers between devices  412 us
    all_to_all x1, waiting for transfers between devices, shards(): lax.all_to_all(jnp.stack([my_group[None]] * lax.axis_size('ka')), 'ka', 0...  138 us
    all_to_all x1, starting transfers between devices, shards(): lax.all_to_all(jnp.stack([my_group[None]] * lax.axis_size('ka')), 'ka', 0...  12.9 us
  transfers between devices with their start and end apart: 3, of which 3 were waited for; matrix products, arithmetic and copies ran while one was open for 0% of the time, Pallas kernels for 0%

profile of v1, /device:TPU:1, one launch (start us, length us, event | category | flops | bytes accessed | tf_op | source)
XLA Modules:
  0.0 618.4 jit_solution(5561305024788096667)
XLA Ops:
  6.5 0.0 copy-start
  6.5 1.4 copy-done
  7.9 0.1 constant_dynamic-slice_fusion.1
  8.0 0.2 copy.19
  8.2 4.4 stack.8
  12.6 0.0 copy-start.1
  12.6 0.0 copy-start.3
  12.6 12.9 %all-to-all-start = ((bf16[32,1,2,20,2400]{4,2,3,1,0:T(2,128)(2,1)}), bf16[32,1,2,20,2400]{4,2,3,1,0:T(2,128)(2,1)}, u32[]{:S(2)}, u32[]{:S(2)}) async-start(bf16[32,1,2,20,2400]{4,2,3,1,0:T(2,128)(2,1)} %stack.8), calls=%async_computation | async-start | bytes 12451840 | tf_op jit(solution)/shard_map/all_to_all | solution.py:25
  25.5 0.0 all-reduce.5.cloned.1.call-start
  25.6 0.7 dynamic-slice_bitcast_fusion
  26.3 0.0 copy-done.1
  26.3 0.1 cosine_multiply_fusion
  26.4 0.0 copy-done.3
  26.4 0.2 fusion
  26.6 138.4 %all-to-all-done = bf16[32,1,2,20,2400]{4,2,3,1,0:T(2,128)(2,1)} async-done(((bf16[32,1,2,20,2400]{4,2,3,1,0:T(2,128)(2,1)}), bf16[32,1,2,20,2400]{4,2,3,1,0:T(2,128)(2,1)}, u32[]{:S(2)}, u32[]{:S(2)}) %all-to-all-start) | async-done | bytes 6144032 | tf_op jit(solution)/shard_map/all_to_all | solution.py:25
  165.0 3.5 copy.13
  168.5 3.5 fusion.24
  172.0 0.3 fusion.11
  172.3 0.3 fusion.21
  172.5 2.5 convolution_bitcast_fusion
  175.0 0.2 fusion.23
  175.2 6.8 %multiply_subtract_fusion = (f32[2,1,160,2400]{3,1,2,0:T(1,128)S(1)}, f32[2,1,160,2400]{3,1,2,0:T(1,128)}) fusion(f32[160,2400]{1,0:T(8,128)S(1)} %get-tuple-element.12, f32[160,2400]{1,0:T(8,128)S(1)} %get-tuple-element.11, f32[2]{0:T(128)S(1)} %sine_multiply_fusion, f32[2]{0:T(128)S(1)} %get-tuple-element.5), kind=kLoop, calls=%fused_computation.3 | loop fusion | flops 4608000 | bytes 9216016 | tf_op jit(solution)/shard_map/sub | solution.py:46
  182.0 10.2 %pad_maximum_fusion = f32[2,2,160,2400]{3,1,2,0:T(2,128)} fusion(f32[2,1,160,2400]{3,1,2,0:T(1,128)} %get-tuple-element.10, f32[2,1,160,2400]{3,1,2,0:T(1,128)S(1)} %get-tuple-element.9), kind=kLoop, calls=%fused_computation | loop fusion | flops 1536000 | bytes 12288000 | tf_op jit(solution)/shard_map/stack | solution.py:46
  192.2 0.0 copy-start.5
  192.2 0.0 copy-start.4
  192.2 0.0 copy-start.2
  192.2 0.0 all-reduce.5.cloned.1.call-update
  192.2 0.0 all-reduce.7.cloned.1.call-start
  192.3 0.6 copy-done.5
  192.9 0.6 dynamic-slice.1
  194.1 146.9 %all-reduce.5.cloned.1.call-done = f32[2,2,160,2400]{3,1,2,0:T(2,128)} async-done(((f32[2,2,160,2400]{3,1,2,0:T(2,128)}), f32[2,2,160,2400]{3,1,2,0:T(2,128)}) %all-reduce.5.cloned.1.call-update) | async-done | bytes 6144016
  341.0 2.1 constant_dynamic-slice_fusion
  343.1 0.0 all-reduce.7.cloned.1.call-update
  343.1 0.0 copy-done.4
  343.1 0.6 dynamic-slice.3
  344.4 0.0 copy-done.2
  344.4 0.1 convolution_bitcast_fusion.1
  344.5 265.5 %all-reduce.7.cloned.1.call-done = f32[2,2,20,2400]{3,1,2,0:T(2,128)} async-done(((f32[2,2,20,2400]{3,1,2,0:T(2,128)}), f32[2,2,20,2400]{3,1,2,0:T(2,128)}) %all-reduce.7.cloned.1.call-update) | async-done | bytes 768016
  610.0 1.6 dynamic-slice_multiply_fusion
  (2 shorter events, 0.1 us)
Async XLA Ops:
  6.5 1.4 copy-start
  12.6 13.7 %copy-start.1 = (s32[2]{0:T(128)S(1)}, s32[2]{0:T(128)}, u32[]{:S(2)}) copy-start(s32[2]{0:T(128)} %param.8) | copy-start | bytes 28
  12.6 13.8 %copy-start.3 = (f32[32]{0:T(128)S(1)}, f32[32]{0:T(128)}, u32[]{:S(2)}) copy-start(f32[32]{0:T(128)} %param.6) | copy-start | bytes 388
  12.6 152.4 %all-to-all-start = ((bf16[32,1,2,20,2400]{4,2,3,1,0:T(2,128)(2,1)}), bf16[32,1,2,20,2400]{4,2,3,1,0:T(2,128)(2,1)}, u32[]{:S(2)}, u32[]{:S(2)}) async-start(bf16[32,1,2,20,2400]{4,2,3,1,0:T(2,128)(2,1)} %stack.8), calls=%async_computation | async-start | bytes 12451840 | tf_op jit(solution)/shard_map/all_to_all | solution.py:25
  25.5 315.4 %all-reduce.5.cloned.1.call-start = ((), (), s32[]{:S(2)}) async-start(), calls=%async_computation.1 | async-start | bytes 12451840
  192.2 0.7 copy-start.5
  192.2 150.9 %copy-start.4 = (u32[256]{0:T(256)S(1)}, u32[256]{0:T(256)}, u32[]{:S(2)}) copy-start(u32[256]{0:T(256)} %constant.64) | copy-start | bytes 3076
  192.2 152.2 %copy-start.2 = (s32[2,30]{1,0:T(2,128)S(1)}, s32[2,30]{1,0:T(2,128)}, u32[]{:S(2)}) copy-start(s32[2,30]{1,0:T(2,128)} %param.9) | copy-start | bytes 724
  192.2 417.8 %all-reduce.7.cloned.1.call-start = ((), (), s32[]{:S(2)}) async-start(), calls=%async_computation.2 | async-start | bytes 1556480
Sparse Core Ops, SparseCore 0:
  192.3 148.5 all-reduce.4
  343.8 266.1 all-reduce.6
